TPU v7x, 256 devices: a whole 4x4x8 slice. The times are simulated.
256 devices in a mesh: scen: 16 (over z, x_lo), pt: 16 (over x_hi, y, core).
Axes of the slice: x: 4 (x_hi: 2, x_lo: 2; x = x_hi * 2 + x_lo), y: 4, z: 8, core: 2. Of those that a mesh axis runs over, the one named last changes fastest.
Arguments:
- slip_counts: int32 [2048, 2048], P('scen'), may hold values from 0 to 7
- spectra: bfloat16 [2048, 4, 4096], P('scen', None, 'pt'), may hold values from -0.125 to 0.125
- transfer: bfloat16 [4096, 4, 2048], P('pt', None, 'scen'), may hold values from -0.09375 to 0.09375
- coast_owner: int32 [2048], P('pt'), may hold values from 0 to 127
Outputs:
- coast: bfloat16 [2048, 4, 2048], P('scen', None, 'pt')
- region_energy: float32 [2048, 128], P('scen')
All inputs are finite; a program needn't handle non-finite values.
Results may differ from a plain program's by a relative error of at most 0.015.
Values may be sent and summed in bfloat16 or wider, within the bound.
A program may use at most 64 MiB of HBM per device.

v0:
```python
import jax
import jax.numpy as jnp
from jax import lax
from jax.sharding import PartitionSpec as P

C = 2048
REGIONS = 128


slip_step = 0.25


def coast_block(field_block, trans_block):
    outputs = []
    for freq in range(2):
        field_re = field_block[:, 2 * freq, :]
        field_im = field_block[:, 2 * freq + 1, :]
        real_left = jnp.stack([field_re, -field_im], axis=-1)
        imag_left = jnp.stack([field_im, field_re], axis=-1)
        left_both = jnp.stack([real_left, imag_left], axis=0)
        trans_pair = trans_block[:, 2 * freq : 2 * freq + 2, :]
        product = jnp.einsum(
            "xspc,pcd->sxd", left_both, trans_pair, preferred_element_type=jnp.float32
        )
        outputs.append(product)
    return jnp.concatenate(outputs, axis=1)


def per_device(slip_counts, spectra, transfer, coast_owner):
    weights = (slip_counts.astype(jnp.float32) * slip_step).astype(jnp.bfloat16)
    scen_rows = weights.shape[0]
    comps = spectra.shape[1]
    local_points = spectra.shape[2]
    piece = lax.all_gather(spectra, "scen", axis=0, tiled=True)
    flat_piece = piece.reshape(piece.shape[0], comps * local_points)
    field_sum = jnp.dot(weights, flat_piece, preferred_element_type=jnp.float32)
    field = field_sum.astype(jnp.bfloat16).reshape(scen_rows, comps, local_points)
    trans_whole = lax.all_gather(transfer, "scen", axis=2, tiled=True)
    partial_sum = coast_block(field, trans_whole)
    coast_sum = lax.psum_scatter(
        partial_sum.astype(jnp.bfloat16), "pt", scatter_dimension=2, tiled=True
    ).astype(jnp.float32)
    coast = coast_sum.astype(jnp.bfloat16)
    squares = jnp.sum(coast_sum * coast_sum, axis=1)
    onehot = (coast_owner[:, None] == jnp.arange(REGIONS, dtype=jnp.int32)[None, :]).astype(
        jnp.float32
    )
    local_energy = jnp.dot(
        squares, onehot, precision=lax.Precision.HIGHEST, preferred_element_type=jnp.float32
    )
    energy = lax.psum(local_energy.astype(jnp.bfloat16), "pt").astype(jnp.float32)
    return (coast, energy * (REGIONS / C))


def solution(mesh):
    placed = (P("scen", None), P("scen", None, "pt"), P("pt", None, "scen"), P("pt"))
    return jax.shard_map(
        per_device,
        mesh=mesh,
        in_specs=placed,
        out_specs=(P("scen", None, "pt"), P("scen", None)),
        check_vma=False,
    )
```

profile of v0, /device:TPU:1, one launch (start us, length us, event | category | flops | bytes accessed | tf_op | source)
XLA Modules:
  0.0 392.1 jit_solution(5593497343896343336)
XLA Ops:
  7.2 0.0 all-gather.3.cloned.1.call-start
  7.2 0.7 all-gather.3.cloned.1.call-update
  7.9 0.0 all-gather.5.cloned.1.call-start
  7.9 1.7 copy.14
  9.7 0.0 all-gather.5.cloned.1.call-update
  9.7 0.0 reduce-scatter.4.cloned.1.call-start
  9.7 100.5 %all-gather.3.cloned.1.call-done = bf16[2048,4,256]{2,1,0:T(4,128)(2,1)} async-done(((bf16[128,4,256]{2,1,0:T(4,128)(2,1)}), bf16[2048,4,256]{2,1,0:T(4,128)(2,1)}) %all-gather.3.cloned.1.call-update) | async-done | bytes 4194320 | tf_op jit(solution)/shard_map/all_gather | solution.py:34
  110.2 0.0 copy-start
  110.2 3.3 copy.27
  113.6 0.0 copy-done
  113.6 0.7 convolution_convert_fusion
  114.3 0.2 reshape.32
  114.5 0.4 fusion.17
  115.0 108.4 %all-gather.5.cloned.1.call-done = bf16[256,4,2048]{2,0,1:T(8,128)(2,1)} async-done(((bf16[256,4,128]{2,0,1:T(8,128)(2,1)}), bf16[256,4,2048]{2,0,1:T(8,128)(2,1)}) %all-gather.5.cloned.1.call-update) | async-done | bytes 4194320 | tf_op jit(solution)/shard_map/all_gather | solution.py:38
  223.4 2.3 fusion.3
  225.7 2.3 fusion.2
  228.0 0.2 pad_maximum_fusion
  228.2 2.5 copy.20
  230.8 3.3 copy.36
  234.1 0.0 copy-start.1
  234.1 0.0 reduce-scatter.4.cloned.1.call-update
  234.1 86.9 %reduce-scatter.4.cloned.1.call-done = bf16[128,512]{1,0:T(8,128)(2,1)} async-done(((bf16[2048,512]{1,0:T(8,128)(2,1)}), bf16[128,512]{1,0:T(8,128)(2,1)}) %reduce-scatter.4.cloned.1.call-update) | async-done | bytes 131088
  321.0 0.9 reshape.38
  322.0 0.8 copy.17
  322.8 0.1 copy.21
  322.9 0.0 copy-done.1
  323.0 0.2 convolution_convert_fusion.1
  323.2 61.7 %psum.7 = bf16[128,128]{1,0:T(8,128)(2,1)S(1)} all-reduce(bf16[128,128]{1,0:T(8,128)(2,1)S(1)} %convolution_convert_fusion.1), channel_id=1, replica_groups=mesh['scen'=16,'pt'=16] {'pt'}, use_global_device_ids=true, to_apply=%region_2.0 | all-reduce | flops 16384 | bytes 65536 | tf_op jit(solution)/shard_map/psum | solution.py:51
  384.9 0.6 convert_multiply_fusion
  (5 shorter events, 0.1 us)
Async XLA Ops:
  7.2 103.1 %all-gather.3.cloned.1.call-start = ((), (), s32[]{:S(2)}) async-start(), calls=%async_computation.1 | async-start | bytes 4456448 | tf_op jit(solution)/shard_map/all_gather | solution.py:34
  7.9 215.5 %all-gather.5.cloned.1.call-start = ((), (), s32[]{:S(2)}) async-start(), calls=%async_computation.2 | async-start | bytes 4456448 | tf_op jit(solution)/shard_map/all_gather | solution.py:38
  9.7 311.3 %reduce-scatter.4.cloned.1.call-start = ((), (), s32[]{:S(2)}) async-start(), calls=%async_computation.3 | async-start | bytes 2228224
  110.2 3.3 copy-start
  234.1 88.9 %copy-start.1 = (s32[128]{0:T(128)S(1)}, s32[128]{0:T(128)}, u32[]{:S(2)}) copy-start(s32[128]{0:T(128)} %param.7) | copy-start | bytes 1540
Sparse Core Ops, SparseCore 0:
  9.8 100.4 all-gather.2
  112.0 111.4 all-gather.4
  234.2 86.7 reduce-scatter.3
where the time goes:
time: 396 us; the launch traced here: 392 us
  waiting for transfers between devices  297 us (75%)
  blocking collectives  61.7 us (16%)
  between operations  13.9 us (4%)
  local copies, waits for them, and re-layouts  13.3 us (3%)
  matrix products  5.58 us (1%)
    all_gather x1, waiting for transfers between devices, per_device(): trans_whole = lax.all_gather(transfer, 'scen', axis=2, tiled=True)  108 us
    all_gather x1, waiting for transfers between devices, per_device(): piece = lax.all_gather(spectra, 'scen', axis=0, tiled=True)  101 us
    unnamed x4, waiting for transfers between devices  87.6 us
    psum x1, blocking collectives, per_device(): lax.psum(local_energy.astype(jnp.bfloat16), 'pt').astype(jnp.float32)  61.7 us
    unnamed x11, local copies, waits for them, and re-layouts  12.7 us
  transfers between devices with their start and end apart: 3, of which 3 were waited for; matrix products, arithmetic and copies ran while one was open for 2% of the time, Pallas kernels for 0%

commit v1 on v0

v1 whole, which is shorter than its diff:
```python
import jax
import jax.numpy as jnp
from jax import lax
from jax.experimental import pallas as pl
from jax.experimental.pallas import tpu as pltpu
from jax.sharding import PartitionSpec as P

REGIONS = 128
SLIP_STEP = 0.25
NZ = 8
NY = 4
N_PT = 16
BF16 = jnp.bfloat16
F32 = jnp.float32
MESH = pl.DeviceIdType.MESH


def kernel(
    slip_ref, x_ref, t_ref, owner_ref, coast_ref, energy_ref,
    xr, tt, wb, gp, ry, rx, sx, hx, ga, acc, ob, co, en, eb, es, eo,
    s_first, s_ring, s_w, s_part, s_xh, s_gring, s_out, s_e, s_f, s_local,
    r_x, r_t, r_w, r_y, r_xh, r_g, r_c, r_e, r_f,
):
    i = lax.axis_index("scen")
    j = lax.axis_index("pt")
    z, xl = i // 2, lax.rem(i, 2)
    xh, y, f = j // 8, lax.rem(j // 2, 4), lax.rem(j, 2)
    g = 1 - f
    up, down = lax.rem(z + 1, NZ), lax.rem(z + NZ - 1, NZ)
    i_up, i_down, i_x = up * 2 + xl, down * 2 + xl, z * 2 + 1 - xl
    j_core = j - f + g
    j_xh = (1 - xh) * 8 + y * 2 + f

    barrier = pltpu.get_barrier_semaphore()

    def greet(a, b):
        pl.semaphore_signal(barrier, inc=1, device_id=(a, b), device_id_type=MESH)

    for a in (i_up, i_down, i_x):
        greet(a, j)
        greet(a, j_core)

    @pl.loop(1, N_PT)
    def _(d):
        greet(i, lax.rem(j + d, N_PT))

    pl.semaphore_wait(barrier, 6 + N_PT - 1)

    def remote(src, dst, s_sem, r_sem, a, b):
        return pltpu.make_async_remote_copy(
            src_ref=src, dst_ref=dst, send_sem=s_sem, recv_sem=r_sem,
            device_id=(a, b), device_id_type=MESH,
        )

    def arrived(dst, r_sem):
        remote(dst, dst, s_local.at[0], r_sem, i, j_core).wait_recv()

    first = [
        remote(t_ref.at[f], tt.at[7, f], s_first.at[0], r_t.at[7, f], i_up, j),
        remote(t_ref.at[f], tt.at[1, f], s_first.at[1], r_t.at[1, f], i_down, j),
        remote(t_ref.at[g], tt.at[7, f], s_first.at[2], r_t.at[7, f], i_up, j_core),
        remote(t_ref.at[g], tt.at[1, f], s_first.at[3], r_t.at[1, f], i_down, j_core),
        remote(x_ref.at[f], xr.at[xl, f], s_first.at[4], r_x.at[xl, f], i_x, j),
        remote(x_ref.at[g], xr.at[xl, f], s_first.at[5], r_x.at[xl, f], i_x, j_core),
        remote(x_ref.at[g], xr.at[xl, f], s_first.at[6], r_x.at[xl, f], i, j_core),
        remote(t_ref.at[g], tt.at[0, f], s_first.at[7], r_t.at[0, f], i, j_core),
    ]
    for copy in first:
        copy.start()
    local = [
        pltpu.make_async_copy(x_ref.at[f], xr.at[xl, f], s_local.at[1]),
        pltpu.make_async_copy(t_ref.at[f], tt.at[0, f], s_local.at[2]),
    ]
    for copy in local:
        copy.start()

    for block in range(NZ):
        counts = slip_ref[:, block * 256 : (block + 1) * 256]
        wb[xl, block] = (counts.astype(F32) * SLIP_STEP).astype(BF16)
    w_copy = remote(wb.at[xl], wb.at[xl], s_w.at[0], r_w.at[0], i_x, j)
    w_copy.start()

    for copy in local:
        copy.wait()
    arrived(xr.at[xl, g], r_x.at[xl, g])
    arrived(xr.at[1 - xl, 0], r_x.at[1 - xl, 0])
    arrived(xr.at[1 - xl, 1], r_x.at[1 - xl, 1])
    arrived(tt.at[0, g], r_t.at[0, g])

    def part_copy(slot):
        owner = lax.rem(z + slot, NZ)
        owner_y, owner_xh = lax.rem(owner, NY), owner // NY
        place = lax.rem(y - owner_y + NY, NY) - 1
        place = jnp.maximum(place, 0)
        return owner_y != y, remote(
            gp.at[slot], ry.at[owner_xh, place], s_part.at[slot], r_y.at[owner_xh, place],
            i, xh * 8 + owner_y * 2 + f,
        )

    def transfer_product(slot):
        for half in range(2):
            prod = jnp.dot(
                xr[half, 0].reshape(256, 256), tt[slot, 0], preferred_element_type=F32
            ) + jnp.dot(xr[half, 1].reshape(256, 256), tt[slot, 1], preferred_element_type=F32)
            rows = slice(half * 128, half * 128 + 128)
            gp[slot, rows, 0:128] = (prod[:128, :128] - prod[128:, 128:]).astype(BF16)
            gp[slot, rows, 128:256] = (prod[:128, 128:] + prod[128:, :128]).astype(BF16)
        away, copy = part_copy(slot)

        @pl.when(away)
        def _():
            copy.start()

    def ring(buf, r_sem, s_sem, use):
        sent = []

        def forward(src_slot, dst_slot, piece, a, n):
            copy = remote(
                buf.at[src_slot, piece], buf.at[dst_slot, piece],
                s_sem.at[n], r_sem.at[dst_slot, piece], a, j,
            )
            copy.start()
            sent.append(copy)

        n = 0
        for step in range(1, 4):
            for piece in range(2):
                for slot, ahead, a in ((8 - step, 7 - step, i_up), (step, step + 1, i_down)):
                    arrived(buf.at[slot, piece], r_sem.at[slot, piece])
                    if step < 3 or piece == (0 if slot > 4 else 1):
                        forward(slot, ahead, piece, a, n)
                        n += 1
            use(8 - step)
            use(step)
        for piece in range(2):
            arrived(buf.at[4, piece], r_sem.at[4, piece])
        use(4)
        return sent

    transfer_product(0)
    sent = ring(tt, r_t, s_ring, transfer_product)

    def summed(h):
        for k in range(NY - 1):
            arrived(ry.at[h, k], r_y.at[h, k])
        own = lax.rem(h * NY + y - z + NZ, NZ)
        total = gp[own].astype(F32)
        for k in range(NY - 1):
            total = total + ry[h, k].astype(F32)
        return total

    sx[...] = summed(1 - xh).astype(BF16)
    xh_copy = remote(sx, rx, s_xh.at[0], r_xh.at[0], i, j_xh)
    xh_copy.start()
    hx[...] = summed(xh)
    arrived(rx, r_xh.at[0])
    for half in range(2):
        rows = slice(half * 128, half * 128 + 128)
        ga[0, half] = (hx[rows, :] + rx[rows, :].astype(F32)).astype(BF16)
    g_first = []
    for half in range(2):
        g_first.append(
            remote(ga.at[0, half], ga.at[7, half], s_gring.at[10 + half], r_g.at[7, half], i_up, j)
        )
        g_first.append(
            remote(ga.at[0, half], ga.at[1, half], s_gring.at[12 + half], r_g.at[1, half], i_down, j)
        )
    for copy in g_first:
        copy.start()

    arrived(wb.at[1 - xl], r_w.at[0])

    def weigh(slot, fresh=False):
        block = lax.rem(z + slot, NZ)
        for half in range(2):
            prod = jnp.dot(
                wb[half, block], ga[slot].reshape(256, 256), preferred_element_type=F32
            )
            if fresh:
                acc[half] = prod
            else:
                acc[half] += prod

    weigh(0, fresh=True)
    sent += ring(ga, r_g, s_gring, weigh)

    for half in range(2):
        ob[half] = acc[half].astype(BF16)
    j_out = xh * 8 + y * 2 + xl
    out_far = remote(ob.at[1 - xl], co.at[f], s_out.at[0], r_c.at[f], i_x, j_out)
    out_far.start()
    out_near = remote(ob.at[xl], co.at[f], s_out.at[1], r_c.at[f], i, j_core)

    @pl.when(f != xl)
    def _():
        out_near.start()
        arrived(co.at[f], r_c.at[f])

    @pl.when(f == xl)
    def _():
        co[f] = ob[xl]

    arrived(co.at[g], r_c.at[g])

    squares = jnp.zeros((128, 128), F32)
    for freq in range(2):
        part = co[freq]
        coast_ref[:, freq * 256 : freq * 256 + 256] = part
        wide = part.astype(F32)
        squares = squares + wide[:, :128] * wide[:, :128] + wide[:, 128:] * wide[:, 128:]
    region = lax.broadcasted_iota(jnp.int32, (REGIONS, 128), 0)
    onehot = (owner_ref[...] == region).astype(F32)
    en[...] = lax.dot_general(
        squares, onehot, (((1,), (1,)), ((), ())),
        precision=lax.Precision.HIGHEST, preferred_element_type=F32,
    ).reshape(N_PT, 8, 128)

    def e_copy(d):
        b = lax.rem(j + d, N_PT)
        return remote(en.at[b], eb.at[j], s_e.at[d], r_e.at[j], i, b)

    def f_copy(d):
        return remote(es, eo.at[j], s_f.at[d], r_f.at[j], i, lax.rem(j + d, N_PT))

    @pl.loop(1, N_PT)
    def _(d):
        e_copy(d).start()

    eb[j] = en[j]

    @pl.loop(1, N_PT)
    def _(d):
        b = lax.rem(j + d, N_PT)
        arrived(eb.at[b], r_e.at[b])

    es[...] = jnp.sum(eb[...], axis=0) * (REGIONS / 2048)

    @pl.loop(1, N_PT)
    def _(d):
        f_copy(d).start()

    eo[j] = es[...]

    @pl.loop(1, N_PT)
    def _(d):
        b = lax.rem(j + d, N_PT)
        arrived(eo.at[b], r_f.at[b])

    energy_ref[...] = eo[...].reshape(128, REGIONS)

    for copy in first + [w_copy] + sent + [xh_copy] + g_first + [out_far]:
        copy.wait_send()
    for slot in range(NZ):
        away, copy = part_copy(slot)

        @pl.when(away)
        def _():
            copy.wait_send()

    @pl.when(f != xl)
    def _():
        out_near.wait_send()

    @pl.loop(1, N_PT)
    def _(d):
        e_copy(d).wait_send()
        f_copy(d).wait_send()


def per_device(slip_counts, spectra, transfer, coast_owner):
    x = spectra.reshape(128, 2, 2, 256).transpose(1, 2, 0, 3)
    t = transfer.reshape(256, 2, 256).transpose(1, 0, 2)
    owner = coast_owner.reshape(1, 128)
    vmem = pl.BlockSpec(memory_space=pltpu.VMEM)
    dma = pltpu.SemaphoreType.DMA
    coast, energy = pl.pallas_call(
        kernel,
        out_shape=(
            jax.ShapeDtypeStruct((128, 512), BF16),
            jax.ShapeDtypeStruct((128, REGIONS), F32),
        ),
        in_specs=[vmem] * 4,
        out_specs=[vmem] * 2,
        scratch_shapes=[
            pltpu.VMEM((2, 2, 2, 128, 256), BF16),
            pltpu.VMEM((NZ, 2, 256, 256), BF16),
            pltpu.VMEM((2, NZ, 128, 256), BF16),
            pltpu.VMEM((NZ, 256, 256), BF16),
            pltpu.VMEM((2, NY - 1, 256, 256), BF16),
            pltpu.VMEM((256, 256), BF16),
            pltpu.VMEM((256, 256), BF16),
            pltpu.VMEM((256, 256), F32),
            pltpu.VMEM((NZ, 2, 128, 256), BF16),
            pltpu.VMEM((2, 128, 256), F32),
            pltpu.VMEM((2, 128, 256), BF16),
            pltpu.VMEM((2, 128, 256), BF16),
            pltpu.VMEM((N_PT, 8, 128), F32),
            pltpu.VMEM((N_PT, 8, 128), F32),
            pltpu.VMEM((8, 128), F32),
            pltpu.VMEM((N_PT, 8, 128), F32),
            dma((8,)),
            dma((10,)),
            dma((1,)),
            dma((NZ,)),
            dma((1,)),
            dma((14,)),
            dma((2,)),
            dma((N_PT,)),
            dma((N_PT,)),
            dma((3,)),
            dma((2, 2)),
            dma((NZ, 2)),
            dma((1,)),
            dma((2, NY - 1)),
            dma((1,)),
            dma((NZ, 2)),
            dma((2,)),
            dma((N_PT,)),
            dma((N_PT,)),
        ],
        compiler_params=pltpu.CompilerParams(collective_id=0, has_side_effects=True),
    )(slip_counts, x, t, owner)
    return coast.reshape(128, 4, 128), energy


def solution(mesh):
    placed = (P("scen", None), P("scen", None, "pt"), P("pt", None, "scen"), P("pt"))
    return jax.shard_map(
        per_device,
        mesh=mesh,
        in_specs=placed,
        out_specs=(P("scen", None, "pt"), P("scen", None)),
        check_vma=False,
    )
```

time: 396 us -> 88.3 us (0.22)
  waiting for transfers between devices: 297 us -> 0 us
  Pallas kernels: 0 us -> 81.3 us
  blocking collectives: 61.7 us -> 0 us
  between operations: 13.9 us -> 0.66 us
  local copies, waits for them, and re-layouts: 13.3 us -> 5.02 us
  matrix products: 5.58 us -> 0 us
    all_gather x2 -> x0, waiting for transfers between devices: 209 us -> none  [the longest x1 108 us: per_device(): trans_whole = lax.all_gather(transfer, 'scen', axis=2, tiled=True)]
    unnamed x4 -> x0, waiting for transfers between devices: 87.6 us -> none
    pallas_call x0 -> x1, Pallas kernels: none -> 81.3 us  [per_device(): pl.pallas_call(kernel, out_shape=(jax.ShapeDtypeStruct((128, 512), BF16),...]
    psum x1 -> x0, blocking collectives: 61.7 us -> none  [per_device(): lax.psum(local_energy.astype(jnp.bfloat16), 'pt').astype(jnp.float32)]
    unnamed x11 -> x7, local copies, waits for them, and re-layouts: 12.7 us -> 2.55 us
    dot_general x4 -> x0, matrix products: 5.58 us -> none  [the longest x2 4.6 us: coast_block(): jnp.einsum('xspc,pcd->sxd', left_both, trans_pair, preferred_element_type...]
  transfers between devices with their start and end apart: 3 -> 0, of which waited for: 3 -> 0; matrix products, arithmetic and copies ran while one was open for 2% -> 0% of each run, Pallas kernels for 0% -> 0%
where the time goes in v1:
time: 88.3 us; the launch traced here: 87 us
  Pallas kernels  81.3 us (92%)
  local copies, waits for them, and re-layouts  5.02 us (6%)
    pallas_call x1, Pallas kernels, per_device(): pl.pallas_call(kernel, out_shape=(jax.ShapeDtypeStruct((128, 512), BF16),...  81.3 us
    unnamed x7, local copies, waits for them, and re-layouts  2.55 us

profile of v1, /device:TPU:1, one launch (start us, length us, event | category | flops | bytes accessed | tf_op | source)
XLA Modules:
  0.0 87.0 jit_solution(6300205816609259992)
XLA Ops:
  0.6 1.1 %copy.8 = bf16[256,4,128]{0,2,1:T(8,128)(2,1)S(1)} copy(bf16[256,4,128]{2,1,0:T(4,128)(2,1)} %param.6) | data formatting | bytes 524288 | tf_op args[2]
  1.7 0.0 copy-start
  1.7 0.8 copy.9
  2.6 0.1 copy-done
  2.7 0.7 copy.7
  3.4 81.3 %shard_map.59 = (bf16[128,512]{1,0:T(8,128)(2,1)}, f32[128,128]{1,0:T(8,128)}) custom-call(s32[128,2048]{1,0:T(8,128)} %slip_ref.1, bf16[2,2,128,256]{3,2,1,0:T(8,128)(2,1)} %bitcast.8, bf16[2,256,256]{2,1,0:T(8,128)(2,1)} %bitcast.7, s32[1,128]{1,0:T(1,128)} %bitcast.9), custom_call_target="tpu_custom_call" | custom-call | tf_op jit(solution)/shard_map/pallas_call | solution.py:276
  84.8 0.0 copy-start.1
  84.8 1.6 %reshape.19 = bf16[128,4,128]{2,1,0:T(4,128)(2,1)} reshape(bf16[128,512]{1,0:T(8,128)(2,1)} %get-tuple-element.4) | data formatting | bytes 262144 | tf_op jit(solution)/shard_map/reshape | solution.py:323
  86.4 0.0 copy-done.1
  86.4 0.6 copy.11
Async XLA Ops:
  1.7 1.0 %copy-start = (bf16[128,4,256]{2,1,0:T(4,128)(2,1)S(1)}, bf16[128,4,256]{2,1,0:T(4,128)(2,1)}, u32[]{:S(2)}) copy-start(bf16[128,4,256]{2,1,0:T(4,128)(2,1)} %param.5) | copy-start | bytes 786436
  84.8 1.6 %copy-start.1 = (f32[128,128]{1,0:T(8,128)S(1)}, f32[128,128]{1,0:T(8,128)}, u32[]{:S(2)}) copy-start(f32[128,128]{1,0:T(8,128)} %get-tuple-element.9) | copy-start | bytes 196612

commit v2 on v0

v2 whole, which is shorter than its diff:
```python
import jax
import jax.numpy as jnp
from jax import lax
from jax.experimental import pallas as pl
from jax.experimental.pallas import tpu as pltpu
from jax.sharding import PartitionSpec as P

REGIONS = 128
SLIP_STEP = 0.25
NZ = 8
NY = 4
N_PT = 16
BF16 = jnp.bfloat16
F32 = jnp.float32
MESH = pl.DeviceIdType.MESH


def kernel(
    slip_hbm, x_hbm, t_hbm, owner_ref, coast_ref, energy_ref,
    slip, x_raw, t_raw, xs, ts, xr, tt, wb, gp, ry, rx, sx, hx, ga, acc, ob, co, own,
    en, eb, es, eo,
    s_first, s_ring, s_w, s_part, s_xh, s_gring, s_out, s_e, s_f, s_local,
    r_x, r_t, r_w, r_y, r_xh, r_g, r_c, r_e, r_f, r_own,
):
    i = lax.axis_index("scen")
    j = lax.axis_index("pt")
    z, xl = i // 2, lax.rem(i, 2)
    xh, y, f = j // 8, lax.rem(j // 2, 4), lax.rem(j, 2)
    g = 1 - f
    up, down = lax.rem(z + 1, NZ), lax.rem(z + NZ - 1, NZ)
    i_up, i_down, i_x = up * 2 + xl, down * 2 + xl, z * 2 + 1 - xl
    j_core = j - f + g
    j_xh = (1 - xh) * 8 + y * 2 + f

    barrier = pltpu.get_barrier_semaphore()

    def greet(a, b):
        pl.semaphore_signal(barrier, inc=1, device_id=(a, b), device_id_type=MESH)

    loads = [
        pltpu.make_async_copy(t_hbm, t_raw, s_local.at[3]),
        pltpu.make_async_copy(x_hbm, x_raw, s_local.at[4]),
        pltpu.make_async_copy(slip_hbm, slip, s_local.at[5]),
    ]
    for copy in loads:
        copy.start()
    for a in (i_up, i_down):
        greet(a, j)
        greet(a, j_core)
    greet(i_x, j)

    @pl.loop(1, N_PT)
    def _(d):
        greet(i, lax.rem(j + d, N_PT))
        greet(i_x, lax.rem(j + d, N_PT))

    def remote(src, dst, s_sem, r_sem, a, b):
        return pltpu.make_async_remote_copy(
            src_ref=src, dst_ref=dst, send_sem=s_sem, recv_sem=r_sem,
            device_id=(a, b), device_id_type=MESH,
        )

    def arrived(dst, r_sem):
        remote(dst, dst, s_local.at[0], r_sem, i, j_core).wait_recv()

    loads[0].wait()
    for k in range(4):
        part = t_raw[:, k, :]
        for half in range(2):
            ts[k // 2, half, :, (k % 2) * 128 : (k % 2) * 128 + 128] = part[
                half * 128 : half * 128 + 128
            ]
    loads[1].wait()
    for k in range(4):
        xs[k // 2, k % 2] = x_raw[:, k, :]
    own[f] = owner_ref[...]

    pl.semaphore_wait(barrier, 5 + 2 * (N_PT - 1))

    first = []
    for half in range(2):
        for slot, a in ((7, i_up), (1, i_down)):
            first.append((ts.at[f, half], tt.at[slot, f, half], r_t.at[slot, f, half], a, j))
    for half in range(2):
        for slot, a in ((7, i_up), (1, i_down)):
            first.append((ts.at[g, half], tt.at[slot, f, half], r_t.at[slot, f, half], a, j_core))
    first.append((xs.at[f], xr.at[xl, f], r_x.at[xl, f], i_x, j))
    first.append((xs.at[g], xr.at[xl, f], r_x.at[xl, f], i_x, j_core))
    first.append((xs.at[g], xr.at[xl, f], r_x.at[xl, f], i, j_core))
    for half in range(2):
        first.append((ts.at[g, half], tt.at[0, f, half], r_t.at[0, f, half], i, j_core))
    first.append((own.at[f], own.at[f], r_own.at[0], i, j_core))
    first = [
        remote(src, dst, s_first.at[n], r_sem, a, b)
        for n, (src, dst, r_sem, a, b) in enumerate(first)
    ]
    for copy in first:
        copy.start()
    local = [
        pltpu.make_async_copy(xs.at[f], xr.at[xl, f], s_local.at[1]),
        pltpu.make_async_copy(ts.at[f], tt.at[0, f], s_local.at[2]),
    ]
    for copy in local:
        copy.start()

    loads[2].wait()
    for block in range(NZ):
        counts = slip[:, block * 256 : (block + 1) * 256]
        wb[block, xl] = (counts.astype(F32) * SLIP_STEP).astype(BF16)
    w_copy = remote(wb.at[:, xl], wb.at[:, xl], s_w.at[0], r_w.at[0], i_x, j)
    w_copy.start()

    def part_copy(slot, half):
        owner = lax.rem(z + slot, NZ)
        owner_y, owner_xh = lax.rem(owner, NY), owner // NY
        place = jnp.maximum(lax.rem(y - owner_y + NY, NY) - 1, 0)
        return owner_y != y, remote(
            gp.at[slot, half], ry.at[owner_xh, place, half], s_part.at[slot, half],
            r_y.at[owner_xh, place, half], i, xh * 8 + owner_y * 2 + f,
        )

    def transfer_product(slot):
        for half in range(2):
            prod = jnp.dot(
                xr[half, 0].reshape(256, 256), tt[slot, 0].reshape(256, 256),
                preferred_element_type=F32,
            ) + jnp.dot(
                xr[half, 1].reshape(256, 256), tt[slot, 1].reshape(256, 256),
                preferred_element_type=F32,
            )
            gp[slot, half, :, 0:128] = (prod[:128, :128] - prod[128:, 128:]).astype(BF16)
            gp[slot, half, :, 128:256] = (prod[:128, 128:] + prod[128:, :128]).astype(BF16)
            away, copy = part_copy(slot, half)

            @pl.when(away)
            def _():
                copy.start()

    sent = []

    def forward(buf, r_sem, s_sem, n, src_slot, dst_slot, piece, a):
        copy = remote(
            buf.at[(src_slot,) + piece], buf.at[(dst_slot,) + piece],
            s_sem.at[n], r_sem.at[(dst_slot,) + piece], a, j,
        )
        copy.start()
        sent.append(copy)

    def ring(buf, r_sem, s_sem, pieces, work):
        n = 0
        for step in range(1, 4):
            for k, piece in enumerate(pieces):
                for slot, ahead, a in ((8 - step, 7 - step, i_up), (step, step + 1, i_down)):
                    at = (slot,) + piece
                    arrived(buf.at[at], r_sem.at[at])
                    first_half = k < len(pieces) // 2
                    if step < 3 or first_half == (slot > 4):
                        forward(buf, r_sem, s_sem, n, slot, ahead, piece, a)
                        n += 1
                work(step, k)
        half = len(pieces) // 2
        for k in range(half):
            for piece in (pieces[k], pieces[k + half]):
                at = (4,) + piece
                arrived(buf.at[at], r_sem.at[at])
            work(4, k)

    def transfer_work(step, k):
        if step == 1 and k == 3:
            for copy in local:
                copy.wait()
            arrived(xr.at[xl, g], r_x.at[xl, g])
            for c in range(2):
                arrived(xr.at[1 - xl, c], r_x.at[1 - xl, c])
                arrived(tt.at[0, g, c], r_t.at[0, g, c])
        plan = {
            (2, 0): 0, (2, 1): 7, (2, 3): 1, (3, 1): 6, (3, 3): 2, (4, 0): 5, (4, 1): 3,
        }
        if (step, k) in plan:
            transfer_product(plan[(step, k)])

    ring(tt, r_t, s_ring, [(f, 0), (f, 1), (g, 0), (g, 1)], transfer_work)
    transfer_product(4)

    def summed(h, half):
        for k in range(NY - 1):
            arrived(ry.at[h, k, half], r_y.at[h, k, half])
        mine = lax.rem(h * NY + y - z + NZ, NZ)
        total = gp[mine, half].astype(F32)
        for k in range(NY - 1):
            total = total + ry[h, k, half].astype(F32)
        return total

    xh_copies = []
    for half in range(2):
        sx[half] = summed(1 - xh, half).astype(BF16)
        copy = remote(sx.at[half], rx.at[half], s_xh.at[half], r_xh.at[half], i, j_xh)
        copy.start()
        xh_copies.append(copy)
    for half in range(2):
        hx[half] = summed(xh, half)
    g_first = []
    for half in range(2):
        arrived(rx.at[half], r_xh.at[half])
        for q in range(2):
            p = half * 2 + q
            rows = slice(q * 64, q * 64 + 64)
            ga[0, p] = (hx[half, rows, :] + rx[half, rows, :].astype(F32)).astype(BF16)
            for n, (slot, a) in enumerate(((7, i_up), (1, i_down))):
                copy = remote(
                    ga.at[0, p], ga.at[slot, p], s_gring.at[20 + 2 * p + n], r_g.at[slot, p], a, j
                )
                copy.start()
                g_first.append(copy)

    arrived(wb.at[:, 1 - xl], r_w.at[0])

    def weigh(slot):
        block = lax.rem(z + slot, NZ)
        prod = jnp.dot(
            wb[block].reshape(256, 256), ga[slot].reshape(256, 256), preferred_element_type=F32
        )
        if slot == 0:
            acc[...] = prod
        else:
            acc[...] += prod

    def weigh_work(step, k):
        plan = {(1, 0): 0, (2, 0): 7, (2, 2): 1, (3, 0): 6, (3, 2): 2, (4, 0): 5}
        if (step, k) in plan:
            weigh(plan[(step, k)])

    ring(ga, r_g, s_gring, [(0,), (1,), (2,), (3,)], weigh_work)
    weigh(3)
    weigh(4)

    total = acc[...]
    for half in range(2):
        ob[half] = total[half * 128 : half * 128 + 128].astype(BF16)
    j_out = xh * 8 + y * 2 + xl
    out_far = remote(ob.at[1 - xl], co.at[f], s_out.at[0], r_c.at[f], i_x, j_out)
    out_far.start()
    out_near = remote(ob.at[xl], co.at[f], s_out.at[1], r_c.at[f], i, j_core)

    @pl.when(f != xl)
    def _():
        out_near.start()

    squares = total[:, :128] * total[:, :128] + total[:, 128:] * total[:, 128:]
    region = lax.broadcasted_iota(jnp.int32, (REGIONS, 128), 0)
    arrived(own.at[g], r_own.at[0])
    onehot = (own[xl] == region).astype(F32).astype(BF16)
    top = squares.astype(BF16)
    rest = (squares - top.astype(F32)).astype(BF16)
    dims = (((1,), (1,)), ((), ()))
    energy = lax.dot_general(top, onehot, dims, preferred_element_type=F32) + lax.dot_general(
        rest, onehot, dims, preferred_element_type=F32
    )
    en[...] = energy.reshape(2, N_PT, 8, 128)

    def e_copy(side, d):
        b = lax.rem(j + d, N_PT)
        return remote(
            en.at[jnp.abs(xl - side), b], eb.at[side, j], s_e.at[side, d], r_e.at[side, j],
            z * 2 + jnp.abs(xl - side), b,
        )

    def f_copy(d):
        return remote(es, eo.at[j], s_f.at[d], r_f.at[j], i, lax.rem(j + d, N_PT))

    @pl.loop(1, N_PT)
    def _(d):
        e_copy(0, d).start()
        e_copy(1, d).start()

    e_copy(1, 0).start()
    eb[0, j] = en[xl, j]

    @pl.when(f != xl)
    def _():
        arrived(co.at[f], r_c.at[f])

    @pl.when(f == xl)
    def _():
        co[f] = ob[xl]

    arrived(co.at[g], r_c.at[g])
    for freq in range(2):
        for comp in range(2):
            coast_ref[:, freq * 2 + comp, :] = co[freq, :, comp * 128 : comp * 128 + 128]

    arrived(eb.at[1, j], r_e.at[1, j])

    @pl.loop(1, N_PT)
    def _(d):
        b = lax.rem(j + d, N_PT)
        arrived(eb.at[0, b], r_e.at[0, b])
        arrived(eb.at[1, b], r_e.at[1, b])

    es[...] = jnp.sum(eb[...].reshape(2 * N_PT, 8, 128), axis=0) * (REGIONS / 2048)

    @pl.loop(1, N_PT)
    def _(d):
        f_copy(d).start()

    eo[j] = es[...]
    for copy in first + [w_copy] + sent + xh_copies + g_first + [out_far]:
        copy.wait_send()
    for slot in range(NZ):
        for half in range(2):
            away, copy = part_copy(slot, half)

            @pl.when(away)
            def _():
                copy.wait_send()

    @pl.when(f != xl)
    def _():
        out_near.wait_send()

    e_copy(1, 0).wait_send()

    @pl.loop(1, N_PT)
    def _(d):
        b = lax.rem(j + d, N_PT)
        arrived(eo.at[b], r_f.at[b])

    energy_ref[...] = eo[...].reshape(128, REGIONS)

    @pl.loop(1, N_PT)
    def _(d):
        e_copy(0, d).wait_send()
        e_copy(1, d).wait_send()
        f_copy(d).wait_send()


def per_device(slip_counts, spectra, transfer, coast_owner):
    owner = coast_owner.reshape(1, 128)
    vmem = pl.BlockSpec(memory_space=pltpu.VMEM)
    hbm = pl.BlockSpec(memory_space=pl.ANY)
    dma = pltpu.SemaphoreType.DMA
    coast, energy = pl.pallas_call(
        kernel,
        out_shape=(
            jax.ShapeDtypeStruct((128, 4, 128), BF16),
            jax.ShapeDtypeStruct((128, REGIONS), F32),
        ),
        in_specs=[hbm] * 3 + [vmem],
        out_specs=[vmem] * 2,
        scratch_shapes=[
            pltpu.VMEM((128, 2048), jnp.int32),
            pltpu.VMEM((128, 4, 256), BF16),
            pltpu.VMEM((256, 4, 128), BF16),
            pltpu.VMEM((2, 2, 128, 256), BF16),
            pltpu.VMEM((2, 2, 128, 256), BF16),
            pltpu.VMEM((2, 2, 2, 128, 256), BF16),
            pltpu.VMEM((NZ, 2, 2, 128, 256), BF16),
            pltpu.VMEM((NZ, 2, 128, 256), BF16),
            pltpu.VMEM((NZ, 2, 128, 256), BF16),
            pltpu.VMEM((2, NY - 1, 2, 128, 256), BF16),
            pltpu.VMEM((2, 128, 256), BF16),
            pltpu.VMEM((2, 128, 256), BF16),
            pltpu.VMEM((2, 128, 256), F32),
            pltpu.VMEM((NZ, 4, 64, 256), BF16),
            pltpu.VMEM((256, 256), F32),
            pltpu.VMEM((2, 128, 256), BF16),
            pltpu.VMEM((2, 128, 256), BF16),
            pltpu.VMEM((2, 1, 128), jnp.int32),
            pltpu.VMEM((2, N_PT, 8, 128), F32),
            pltpu.VMEM((2, N_PT, 8, 128), F32),
            pltpu.VMEM((8, 128), F32),
            pltpu.VMEM((N_PT, 8, 128), F32),
            dma((14,)),
            dma((20,)),
            dma((1,)),
            dma((NZ, 2)),
            dma((2,)),
            dma((28,)),
            dma((2,)),
            dma((2, N_PT)),
            dma((N_PT,)),
            dma((6,)),
            dma((2, 2)),
            dma((NZ, 2, 2)),
            dma((1,)),
            dma((2, NY - 1, 2)),
            dma((2,)),
            dma((NZ, 4)),
            dma((2,)),
            dma((2, N_PT)),
            dma((N_PT,)),
            dma((1,)),
        ],
        compiler_params=pltpu.CompilerParams(collective_id=0, has_side_effects=True),
    )(slip_counts, spectra, transfer, owner)
    return coast, energy


def solution(mesh):
    placed = (P("scen", None), P("scen", None, "pt"), P("pt", None, "scen"), P("pt"))
    return jax.shard_map(
        per_device,
        mesh=mesh,
        in_specs=placed,
        out_specs=(P("scen", None, "pt"), P("scen", None)),
        check_vma=False,
    )
```

time: 396 us -> 76.1 us (0.19)
  waiting for transfers between devices: 297 us -> 0 us
  Pallas kernels: 0 us -> 73.1 us
  blocking collectives: 61.7 us -> 0 us
  between operations: 13.9 us -> 0.65 us
  local copies, waits for them, and re-layouts: 13.3 us -> 2.27 us
  matrix products: 5.58 us -> 0 us
    all_gather x2 -> x0, waiting for transfers between devices: 209 us -> none  [the longest x1 108 us: per_device(): trans_whole = lax.all_gather(transfer, 'scen', axis=2, tiled=True)]
    unnamed x4 -> x0, waiting for transfers between devices: 87.6 us -> none
    pallas_call x0 -> x1, Pallas kernels: none -> 73.1 us  [per_device(): pl.pallas_call(kernel, out_shape=(jax.ShapeDtypeStruct((128, 4, 128), BF1...]
    psum x1 -> x0, blocking collectives: 61.7 us -> none  [per_device(): lax.psum(local_energy.astype(jnp.bfloat16), 'pt').astype(jnp.float32)]
    unnamed x11 -> x4, local copies, waits for them, and re-layouts: 12.7 us -> 2.27 us
    dot_general x4 -> x0, matrix products: 5.58 us -> none  [the longest x2 4.6 us: coast_block(): jnp.einsum('xspc,pcd->sxd', left_both, trans_pair, preferred_element_type...]
  transfers between devices with their start and end apart: 3 -> 0, of which waited for: 3 -> 0; matrix products, arithmetic and copies ran while one was open for 2% -> 0% of each run, Pallas kernels for 0% -> 0%
where the time goes in v2:
time: 76.1 us; the launch traced here: 76 us
  Pallas kernels  73.1 us (96%)
  local copies, waits for them, and re-layouts  2.27 us (3%)
    pallas_call x1, Pallas kernels, per_device(): pl.pallas_call(kernel, out_shape=(jax.ShapeDtypeStruct((128, 4, 128), BF1...  73.1 us
    unnamed x4, local copies, waits for them, and re-layouts  2.27 us

profile of v2, /device:TPU:1, one launch (start us, length us, event | category | flops | bytes accessed | tf_op | source)
XLA Modules:
  0.0 76.0 jit_solution(777680431389125668)
XLA Ops:
  0.6 73.1 %shard_map.59 = (bf16[128,4,128]{2,1,0:T(4,128)(2,1)}, f32[128,128]{1,0:T(8,128)}) custom-call(s32[128,2048]{1,0:T(8,128)} %slip_hbm.1, bf16[128,4,256]{2,1,0:T(4,128)(2,1)} %x_hbm.1, bf16[256,4,128]{2,1,0:T(4,128)(2,1)} %t_hbm.1, s32[1,128]{1,0:T(1,128)} %bitcast.1), custom_call_target="tpu_custom_call" | custom-call | tf_op jit(solution)/shard_map/pallas_call | solution.py:342
  73.7 0.0 copy-start
  73.7 1.6 %copy.8 = bf16[128,4,128]{2,1,0:T(4,128)(2,1)} copy(bf16[128,4,128]{2,1,0:T(4,128)(2,1)} %get-tuple-element.4) | data formatting | bytes 262144
  75.4 0.0 copy-done
  75.4 0.6 copy.9
Async XLA Ops:
  73.7 1.6 %copy-start = (f32[128,128]{1,0:T(8,128)S(1)}, f32[128,128]{1,0:T(8,128)}, u32[]{:S(2)}) copy-start(f32[128,128]{1,0:T(8,128)} %get-tuple-element.5) | copy-start | bytes 196612

commit v3 on v2

--- a/solution.py
+++ b/solution.py
@@ -19,7 +19,7 @@
     slip_hbm, x_hbm, t_hbm, owner_ref, coast_ref, energy_ref,
     slip, x_raw, t_raw, xs, ts, xr, tt, wb, gp, ry, rx, sx, hx, ga, acc, ob, co, own,
     en, eb, es, eo,
-    s_first, s_ring, s_w, s_part, s_xh, s_gring, s_out, s_e, s_f, s_local,
+    s_all, s_local,
     r_x, r_t, r_w, r_y, r_xh, r_g, r_c, r_e, r_f, r_own,
 ):
     i = lax.axis_index("scen")
@@ -54,14 +54,14 @@
         greet(i, lax.rem(j + d, N_PT))
         greet(i_x, lax.rem(j + d, N_PT))
 
-    def remote(src, dst, s_sem, r_sem, a, b):
+    def remote(src, dst, r_sem, a, b):
         return pltpu.make_async_remote_copy(
-            src_ref=src, dst_ref=dst, send_sem=s_sem, recv_sem=r_sem,
+            src_ref=src, dst_ref=dst, send_sem=s_all.at[0], recv_sem=r_sem,
             device_id=(a, b), device_id_type=MESH,
         )
 
     def arrived(dst, r_sem):
-        remote(dst, dst, s_local.at[0], r_sem, i, j_core).wait_recv()
+        remote(dst, dst, r_sem, i, j_core).wait_recv()
 
     loads[0].wait()
     for k in range(4):
@@ -91,8 +91,7 @@
         first.append((ts.at[g, half], tt.at[0, f, half], r_t.at[0, f, half], i, j_core))
     first.append((own.at[f], own.at[f], r_own.at[0], i, j_core))
     first = [
-        remote(src, dst, s_first.at[n], r_sem, a, b)
-        for n, (src, dst, r_sem, a, b) in enumerate(first)
+        remote(src, dst, r_sem, a, b) for src, dst, r_sem, a, b in first
     ]
     for copy in first:
         copy.start()
@@ -107,7 +106,7 @@
     for block in range(NZ):
         counts = slip[:, block * 256 : (block + 1) * 256]
         wb[block, xl] = (counts.astype(F32) * SLIP_STEP).astype(BF16)
-    w_copy = remote(wb.at[:, xl], wb.at[:, xl], s_w.at[0], r_w.at[0], i_x, j)
+    w_copy = remote(wb.at[:, xl], wb.at[:, xl], r_w.at[0], i_x, j)
     w_copy.start()
 
     def part_copy(slot, half):
@@ -115,8 +114,8 @@
         owner_y, owner_xh = lax.rem(owner, NY), owner // NY
         place = jnp.maximum(lax.rem(y - owner_y + NY, NY) - 1, 0)
         return owner_y != y, remote(
-            gp.at[slot, half], ry.at[owner_xh, place, half], s_part.at[slot, half],
-            r_y.at[owner_xh, place, half], i, xh * 8 + owner_y * 2 + f,
+            gp.at[slot, half], ry.at[owner_xh, place, half], r_y.at[owner_xh, place, half],
+            i, xh * 8 + owner_y * 2 + f,
         )
 
     def transfer_product(slot):
@@ -138,16 +137,15 @@
 
     sent = []
 
-    def forward(buf, r_sem, s_sem, n, src_slot, dst_slot, piece, a):
+    def forward(buf, r_sem, src_slot, dst_slot, piece, a):
         copy = remote(
             buf.at[(src_slot,) + piece], buf.at[(dst_slot,) + piece],
-            s_sem.at[n], r_sem.at[(dst_slot,) + piece], a, j,
+            r_sem.at[(dst_slot,) + piece], a, j,
         )
         copy.start()
         sent.append(copy)
 
-    def ring(buf, r_sem, s_sem, pieces, work):
-        n = 0
+    def ring(buf, r_sem, pieces, work):
         for step in range(1, 4):
             for k, piece in enumerate(pieces):
                 for slot, ahead, a in ((8 - step, 7 - step, i_up), (step, step + 1, i_down)):
@@ -155,8 +153,7 @@
                     arrived(buf.at[at], r_sem.at[at])
                     first_half = k < len(pieces) // 2
                     if step < 3 or first_half == (slot > 4):
-                        forward(buf, r_sem, s_sem, n, slot, ahead, piece, a)
-                        n += 1
+                        forward(buf, r_sem, slot, ahead, piece, a)
                 work(step, k)
         half = len(pieces) // 2
         for k in range(half):
@@ -179,7 +176,7 @@
         if (step, k) in plan:
             transfer_product(plan[(step, k)])
 
-    ring(tt, r_t, s_ring, [(f, 0), (f, 1), (g, 0), (g, 1)], transfer_work)
+    ring(tt, r_t, [(f, 0), (f, 1), (g, 0), (g, 1)], transfer_work)
     transfer_product(4)
 
     def summed(h, half):
@@ -194,7 +191,7 @@
     xh_copies = []
     for half in range(2):
         sx[half] = summed(1 - xh, half).astype(BF16)
-        copy = remote(sx.at[half], rx.at[half], s_xh.at[half], r_xh.at[half], i, j_xh)
+        copy = remote(sx.at[half], rx.at[half], r_xh.at[half], i, j_xh)
         copy.start()
         xh_copies.append(copy)
     for half in range(2):
@@ -206,10 +203,8 @@
             p = half * 2 + q
             rows = slice(q * 64, q * 64 + 64)
             ga[0, p] = (hx[half, rows, :] + rx[half, rows, :].astype(F32)).astype(BF16)
-            for n, (slot, a) in enumerate(((7, i_up), (1, i_down))):
-                copy = remote(
-                    ga.at[0, p], ga.at[slot, p], s_gring.at[20 + 2 * p + n], r_g.at[slot, p], a, j
-                )
+            for slot, a in ((7, i_up), (1, i_down)):
+                copy = remote(ga.at[0, p], ga.at[slot, p], r_g.at[slot, p], a, j)
                 copy.start()
                 g_first.append(copy)
 
@@ -230,7 +225,7 @@
         if (step, k) in plan:
             weigh(plan[(step, k)])
 
-    ring(ga, r_g, s_gring, [(0,), (1,), (2,), (3,)], weigh_work)
+    ring(ga, r_g, [(0,), (1,), (2,), (3,)], weigh_work)
     weigh(3)
     weigh(4)
 
@@ -238,9 +233,9 @@
     for half in range(2):
         ob[half] = total[half * 128 : half * 128 + 128].astype(BF16)
     j_out = xh * 8 + y * 2 + xl
-    out_far = remote(ob.at[1 - xl], co.at[f], s_out.at[0], r_c.at[f], i_x, j_out)
+    out_far = remote(ob.at[1 - xl], co.at[f], r_c.at[f], i_x, j_out)
     out_far.start()
-    out_near = remote(ob.at[xl], co.at[f], s_out.at[1], r_c.at[f], i, j_core)
+    out_near = remote(ob.at[xl], co.at[f], r_c.at[f], i, j_core)
 
     @pl.when(f != xl)
     def _():
@@ -256,32 +251,34 @@
     energy = lax.dot_general(top, onehot, dims, preferred_element_type=F32) + lax.dot_general(
         rest, onehot, dims, preferred_element_type=F32
     )
-    en[...] = energy.reshape(2, N_PT, 8, 128)
+    en[...] = energy.reshape(2, NZ, 16, 128)
+
+    place = xh * NY + y
 
     def e_copy(side, d):
-        b = lax.rem(j + d, N_PT)
+        h = jnp.abs(xl - side)
+        b = lax.rem(place + d, NZ)
         return remote(
-            en.at[jnp.abs(xl - side), b], eb.at[side, j], s_e.at[side, d], r_e.at[side, j],
-            z * 2 + jnp.abs(xl - side), b,
+            en.at[h, b], eb.at[xl, j], r_e.at[0], z * 2 + h, b * 2 + h
         )
 
-    def f_copy(d):
-        return remote(es, eo.at[j], s_f.at[d], r_f.at[j], i, lax.rem(j + d, N_PT))
-
-    @pl.loop(1, N_PT)
+    e_copy(1, 0).start()
+
+    @pl.loop(1, NZ)
     def _(d):
         e_copy(0, d).start()
         e_copy(1, d).start()
 
-    e_copy(1, 0).start()
-    eb[0, j] = en[xl, j]
+    e_own = pltpu.make_async_copy(en.at[xl, place], eb.at[xl, j], r_e.at[0])
 
     @pl.when(f != xl)
     def _():
+        e_copy(0, 0).start()
         arrived(co.at[f], r_c.at[f])
 
     @pl.when(f == xl)
     def _():
+        e_own.start()
         co[f] = ob[xl]
 
     arrived(co.at[g], r_c.at[g])
@@ -289,49 +286,46 @@
         for comp in range(2):
             coast_ref[:, freq * 2 + comp, :] = co[freq, :, comp * 128 : comp * 128 + 128]
 
-    arrived(eb.at[1, j], r_e.at[1, j])
-
-    @pl.loop(1, N_PT)
-    def _(d):
-        b = lax.rem(j + d, N_PT)
-        arrived(eb.at[0, b], r_e.at[0, b])
-        arrived(eb.at[1, b], r_e.at[1, b])
-
-    es[...] = jnp.sum(eb[...].reshape(2 * N_PT, 8, 128), axis=0) * (REGIONS / 2048)
-
-    @pl.loop(1, N_PT)
-    def _(d):
-        f_copy(d).start()
-
-    eo[j] = es[...]
+    @pl.when(f == xl)
+    def _():
+        pltpu.make_async_copy(eb, eb, r_e.at[0]).wait()
+        es[...] = jnp.sum(eb[...].reshape(2 * N_PT, 16, 128), axis=0) * (REGIONS / 2048)
+
+        @pl.loop(1, N_PT)
+        def _(d):
+            remote(es, eo.at[place], r_f.at[0], i, lax.rem(j + d, N_PT)).start()
+
+        pltpu.make_async_copy(es, eo.at[place], r_f.at[0]).start()
+
     for copy in first + [w_copy] + sent + xh_copies + g_first + [out_far]:
         copy.wait_send()
-    for slot in range(NZ):
+    for slot in range(6):
         for half in range(2):
-            away, copy = part_copy(slot, half)
-
-            @pl.when(away)
-            def _():
-                copy.wait_send()
+            part_copy(slot, half)[1].wait_send()
+
+    def drain(ref):
+        remote(ref, ref, r_f.at[0], i, j_core).wait_send()
+
+    drain(en.at[0])
+    drain(en.at[1, pl.ds(0, 7)])
 
     @pl.when(f != xl)
     def _():
         out_near.wait_send()
-
-    e_copy(1, 0).wait_send()
-
-    @pl.loop(1, N_PT)
-    def _(d):
-        b = lax.rem(j + d, N_PT)
-        arrived(eo.at[b], r_f.at[b])
-
+        drain(es)
+
+    @pl.when(f == xl)
+    def _():
+        drain(en.at[0])
+        drain(en.at[1, pl.ds(0, 7)])
+
+    pltpu.make_async_copy(eo, eo, r_f.at[0]).wait()
     energy_ref[...] = eo[...].reshape(128, REGIONS)
 
-    @pl.loop(1, N_PT)
-    def _(d):
-        e_copy(0, d).wait_send()
-        e_copy(1, d).wait_send()
-        f_copy(d).wait_send()
+
+def settle(coast_in, energy_in, coast_ref, energy_ref):
+    coast_ref[...] = coast_in[...]
+    energy_ref[...] = energy_in[...]
 
 
 def per_device(slip_counts, spectra, transfer, coast_owner):
@@ -366,19 +360,11 @@
             pltpu.VMEM((2, 128, 256), BF16),
             pltpu.VMEM((2, 128, 256), BF16),
             pltpu.VMEM((2, 1, 128), jnp.int32),
-            pltpu.VMEM((2, N_PT, 8, 128), F32),
-            pltpu.VMEM((2, N_PT, 8, 128), F32),
-            pltpu.VMEM((8, 128), F32),
-            pltpu.VMEM((N_PT, 8, 128), F32),
-            dma((14,)),
-            dma((20,)),
+            pltpu.VMEM((2, NZ, 16, 128), F32),
+            pltpu.VMEM((2, N_PT, 16, 128), F32),
+            pltpu.VMEM((16, 128), F32),
+            pltpu.VMEM((NZ, 16, 128), F32),
             dma((1,)),
-            dma((NZ, 2)),
-            dma((2,)),
-            dma((28,)),
-            dma((2,)),
-            dma((2, N_PT)),
-            dma((N_PT,)),
             dma((6,)),
             dma((2, 2)),
             dma((NZ, 2, 2)),
@@ -387,13 +373,21 @@
             dma((2,)),
             dma((NZ, 4)),
             dma((2,)),
-            dma((2, N_PT)),
-            dma((N_PT,)),
+            dma((1,)),
+            dma((1,)),
             dma((1,)),
         ],
         compiler_params=pltpu.CompilerParams(collective_id=0, has_side_effects=True),
     )(slip_counts, spectra, transfer, owner)
-    return coast, energy
+    return pl.pallas_call(
+        settle,
+        out_shape=(
+            jax.ShapeDtypeStruct((128, 4, 128), BF16),
+            jax.ShapeDtypeStruct((128, REGIONS), F32),
+        ),
+        in_specs=[vmem] * 2,
+        out_specs=[vmem] * 2,
+    )(coast, energy)
 
 
 def solution(mesh):

time: 76.1 us -> 73.7 us (0.968)
  local copies, waits for them, and re-layouts: 2.27 us -> 0 us
    unnamed x4 -> x0, local copies, waits for them, and re-layouts: 2.27 us -> none
    pallas_call x1, Pallas kernels: 73.1 us -> 71.4 us  [per_device(): pl.pallas_call(kernel, out_shape=(jax.ShapeDtypeStruct((128, 4, 128), BF1...]
    pallas_call x0 -> x1, Pallas kernels: none -> 1.59 us  [per_device(): pl.pallas_call(settle, out_shape=(jax.ShapeDtypeStruct((128, 4, 128), BF1...]
where the time goes in v3:
time: 73.7 us; the launch traced here: 73.6 us
  Pallas kernels  73 us (99%)
    pallas_call x1, Pallas kernels, per_device(): pl.pallas_call(kernel, out_shape=(jax.ShapeDtypeStruct((128, 4, 128), BF1...  71.4 us
    pallas_call x1, Pallas kernels, per_device(): pl.pallas_call(settle, out_shape=(jax.ShapeDtypeStruct((128, 4, 128), BF1...  1.59 us

profile of v3, /device:TPU:1, one launch (start us, length us, event | category | flops | bytes accessed | tf_op | source)
XLA Modules:
  0.0 73.6 jit_solution(7220236901633756337)
XLA Ops:
  0.6 71.4 %shard_map.59 = (bf16[128,4,128]{2,1,0:T(4,128)(2,1)}, f32[128,128]{1,0:T(8,128)}) custom-call(s32[128,2048]{1,0:T(8,128)} %slip_hbm.1, bf16[128,4,256]{2,1,0:T(4,128)(2,1)} %x_hbm.1, bf16[256,4,128]{2,1,0:T(4,128)(2,1)} %t_hbm.1, s32[1,128]{1,0:T(1,128)} %bitcast.1), custom_call_target="tpu_custom_call" | custom-call | tf_op jit(solution)/shard_map/pallas_call | solution.py:336
  72.0 1.6 %shard_map.60 = (bf16[128,4,128]{2,1,0:T(4,128)(2,1)}, f32[128,128]{1,0:T(8,128)}) custom-call(bf16[128,4,128]{2,1,0:T(4,128)(2,1)} %get-tuple-element.4.coast_in, f32[128,128]{1,0:T(8,128)} %get-tuple-element.5.energy_in), custom_call_target="tpu_custom_call" | custom-call | tf_op jit(solution)/shard_map/pallas_call | solution.py:382
